TPU v7x, 512 devices: a whole 4x4x16 slice. The times are simulated.
512 devices in a mesh: tensor: 8 (over x, core), context: 64 (over y, z).
Axes of the slice: x: 4, y: 4, z: 16, core: 2. Of those that a mesh axis runs over, the one named last changes fastest.
Arguments:
- q_proj: bfloat16 [16384, 8192], P('context', 'tensor'), may hold values from -6 to 6
- k_proj: bfloat16 [16384, 8192], P('context', 'tensor'), may hold values from -6 to 6
- v_proj: bfloat16 [16384, 8192], P('context', 'tensor'), may hold values from -6 to 6
- short_filter: bfloat16 [3, 3, 512], P(None, None, 'tensor'), may hold values from -3.5 to 3.5
- residue: float32 [16, 8192], P(None, 'tensor'), may hold values from -1.5 to 1.5
- decay_rate: float32 [16, 8192], P(None, 'tensor'), may hold values from 0.5 to 512
- out_weight: bfloat16 [4096, 8192], P('context', 'tensor'), may hold values from -0.0625 to 0.0625
Outputs:
- projected: bfloat16 [4096, 16384], P('tensor', 'context')
All inputs are finite; a program needn't handle non-finite values.
Results may differ from a plain program's by a relative error of at most 0.02.
Values may be sent and summed in bfloat16 or wider, within the bound.
A program may use at most 128 MiB of HBM per device.

v0:
```python
import jax
import jax.numpy as jnp
import numpy as np
from jax import lax
from jax.sharding import PartitionSpec as P


def passed_along(block, axis, distance):
    devices = range(lax.axis_size(axis))
    route = [(i - distance, i) for i in devices if i - distance in devices]
    return lax.ppermute(block, axis, route)


def prefix(part, axis, combine, identity):
    place = lax.axis_index(axis)
    gathered = jax.tree.map(lambda a: lax.all_gather(a, axis), part)
    state = jax.tree.map(lambda a, e: jnp.zeros_like(a) + jnp.asarray(e, a.dtype), part, identity)

    def one(lap, state):
        return combine(
            state, jax.tree.map(lambda a: lax.dynamic_index_in_dim(a, lap, 0, False), gathered)
        )

    return lax.fori_loop(0, place, one, state)


def short_pass(extended, filters, group_width):
    tap_count = filters.shape[0]
    length_rows, chan_count = extended.shape
    groups = filters.shape[1]
    widened = jnp.broadcast_to(
        filters.astype(jnp.float32)[:, :, None], (tap_count, groups, group_width)
    ).reshape(tap_count, chan_count)
    out_rows = length_rows - tap_count + 1
    running = jnp.zeros((out_rows, chan_count), jnp.float32)
    for offset in range(tap_count):
        begin = tap_count - 1 - offset
        running = running + widened[offset][None, :] * extended[begin : begin + out_rows].astype(
            jnp.float32
        )
    return running


def compose(earlier, later):
    return (earlier[0] * later[0], earlier[1] * later[0] + later[1])


def per_device(q_proj, k_proj, v_proj, short_filter, residue, decay_rate, out_weight):
    row_count, chan_count = q_proj.shape
    short_taps = short_filter.shape[1]
    group_width = chan_count // short_filter.shape[2]
    lead_rows = short_taps - 1
    q_rim, k_rim, v_rim = passed_along(
        (
            q_proj[row_count - lead_rows :],
            k_proj[row_count - lead_rows :],
            v_proj[row_count - lead_rows :],
        ),
        "context",
        1,
    )
    q_feat = short_pass(
        jnp.concatenate([q_rim, q_proj], axis=0), short_filter[0], group_width
    ).astype(jnp.bfloat16)
    k_feat = short_pass(
        jnp.concatenate([k_rim, k_proj], axis=0), short_filter[1], group_width
    ).astype(jnp.bfloat16)
    v_feat = short_pass(
        jnp.concatenate([v_rim, v_proj], axis=0), short_filter[2], group_width
    ).astype(jnp.bfloat16)
    product = (k_feat.astype(jnp.float32) * v_feat.astype(jnp.float32)).astype(jnp.bfloat16)
    sub_len = 16
    sub_count = row_count // sub_len
    decay_step = decay_rate / (row_count * lax.axis_size("context"))
    mode_scale = residue * jnp.sqrt(2.0 * decay_step)
    offsets = jnp.arange(sub_len).astype(jnp.float32)
    intra_kernel = jnp.sum(
        mode_scale[None] * jnp.exp(-decay_step[None] * offsets[:, None, None]), axis=1
    )
    gap_table = np.arange(sub_len)[None, :] - np.arange(sub_len)[:, None]
    one_hot = (gap_table[:, :, None] == np.arange(sub_len)[None, None, :]).astype(np.float32)
    toeplitz = jnp.einsum(
        "sto,oc->stc", jnp.asarray(one_hot), intra_kernel, precision=lax.Precision.HIGHEST
    )
    local_rows = product.astype(jnp.float32).reshape(sub_count, sub_len, chan_count)
    local_part = jnp.einsum("qsc,stc->qtc", local_rows, toeplitz, precision=lax.Precision.HIGHEST)
    tail_powers = jnp.exp(-decay_step[None] * (sub_len - 1 - offsets)[:, None, None])
    sub_ends = jnp.einsum("qsc,smc->qmc", local_rows, tail_powers, precision=lax.Precision.HIGHEST)
    step_decay = jnp.broadcast_to(jnp.exp(-decay_step * sub_len)[None], sub_ends.shape)
    ignored, carried = lax.associative_scan(compose, (step_decay, sub_ends))
    block_state = carried[-1]
    previous = jnp.concatenate([jnp.zeros_like(carried[:1]), carried[:-1]], axis=0)
    block_decay = jnp.exp(-decay_step * row_count)
    unused, incoming = prefix(
        (block_decay, block_state),
        "context",
        compose,
        (jnp.ones_like(block_decay), jnp.zeros_like(block_state)),
    )
    start_decay = jnp.exp(
        -decay_step[None] * (sub_len * jnp.arange(sub_count)).astype(jnp.float32)[:, None, None]
    )
    prior = previous + start_decay * incoming[None]
    lead_powers = jnp.exp(-decay_step[None] * (offsets + 1.0)[:, None, None])
    carried_part = jnp.einsum(
        "qmc,smc->qsc", prior * mode_scale[None], lead_powers, precision=lax.Precision.HIGHEST
    )
    modal_out = (local_part + carried_part).reshape(row_count, chan_count)
    gated = (q_feat.astype(jnp.float32) * modal_out).astype(jnp.bfloat16)
    partial_terms = lax.dot_general(
        lax.all_gather(out_weight, "context", axis=0, tiled=True),
        gated,
        (((1,), (1,)), ((), ())),
        preferred_element_type=jnp.float32,
    )
    return lax.psum_scatter(
        partial_terms.astype(jnp.bfloat16), "tensor", scatter_dimension=0, tiled=True
    )


def solution(mesh):
    return jax.shard_map(
        per_device,
        mesh=mesh,
        in_specs=(
            P("context", "tensor"),
            P("context", "tensor"),
            P("context", "tensor"),
            P(None, None, "tensor"),
            P(None, "tensor"),
            P(None, "tensor"),
            P("context", "tensor"),
        ),
        out_specs=P("tensor", "context"),
        check_vma=False,
    )
```

profile of v0, /device:TPU:8, one launch (start us, length us, event | category | flops | bytes accessed | tf_op | source)
XLA Modules:
  0.0 510.7 jit_solution(3309768442686726028)
XLA Ops:
  6.5 1.6 multiply_exponential_fusion.2
  8.2 0.7 slice.217
  9.0 3.8 collective-permute-start.1
  12.8 0.7 slice.227
  13.5 3.8 collective-permute-start.2
  17.4 0.7 slice_convert_fusion.2
  19.2 6.2 %copy.86 = f32[16,16,1024]{1,0,2:T(8,128)} copy(f32[16,16,1024]{2,1,0:T(8,128)S(1)} %multiply_exponential_fusion) | data formatting | bytes 2097152 | tf_op jit(solution)/shard_map/exp | solution.py:87
  25.4 0.7 multiply_convert_fusion
  26.2 4.7 copy.85
  30.9 12.5 %fusion.15 = f32[1024,16,16]{1,2,0:T(8,128)} fusion(f32[16,16,1024]{1,0,2:T(8,128)} %copy.86, bf16[16,16,1024]{1,0,2:T(8,128)(2,1)} %copy.85), kind=kOutput, calls=%fused_computation.72 | convolution fusion | flops 50331648 | bytes 2621440 | tf_op jit(solution)/shard_map/qsc,smc->qmc/dot_general | solution.py:88
  43.4 5.2 %copy.88 = f32[1024,16,16]{0,1,2:T(8,128)S(1)} copy(f32[1024,16,16]{1,2,0:T(8,128)} %fusion.15) | data formatting | bytes 2097152 | tf_op jit(solution)/shard_map/qsc,smc->qmc/dot_general | solution.py:88
  49.2 3.5 pad.122
  52.8 1.5 slice.359
  55.0 0.7 slice.207
  55.8 3.8 collective-permute-start
  60.1 3.6 pad.33
  64.0 2.3 slice_add_fusion
  66.3 93.0 %all-gather.9.cloned.1.call-done = f32[1024,1024]{1,0:T(8,128)} async-done(((f32[16,1024]{1,0:T(8,128)}), f32[1024,1024]{1,0:T(8,128)}) %all-gather.9.cloned.1.call-update) | async-done | bytes 4194320 | tf_op jit(solution)/shard_map/all_gather | solution.py:16
  159.3 143.9 %all-gather.5.cloned.1.call-done = f32[64,16,1024]{2,1,0:T(8,128)} async-done(((f32[1,16,1024]{2,1,0:T(8,128)}), f32[64,16,1024]{2,1,0:T(8,128)}) %all-gather.5.cloned.1.call-update) | async-done | bytes 4194320 | tf_op jit(solution)/shard_map/all_gather | solution.py:16
  303.2 15.0 %while.12 = (s32[]{:T(128)}, f32[16,1024]{1,0:T(8,128)S(1)}, s32[]{:T(128)}, f32[64,16,1024]{2,1,0:T(8,128)}, f32[64,16,1024]{2,1,0:T(8,128)}, /*index=5*/s32[]{:T(128)}, s32[]{:T(128)}, s32[]{:T(128)}) while((s32[]{:T(128)}, f32[16,1024]{1,0:T(8,128)S(1)}, s32[]{:T(128)}, f32[64,16,1024]{2,1,0:T(8,128)}, f32[64,16,1024]{2,1,0:T(8,128)}, ...), condition=%wide.region_2.3_spmd, body=%wide.region_1.2_spmd.sunk | while | flops 32773 | bytes 262267 | solution.py:24
  303.2 0.9 bitcast_add_fusion.2
  304.1 0.9 bitcast_add_fusion.2
  305.0 0.9 bitcast_add_fusion.2
  306.0 0.9 bitcast_add_fusion.2
  306.9 0.9 bitcast_add_fusion.2
  307.8 0.9 bitcast_add_fusion.2
  308.7 0.9 bitcast_add_fusion.2
  309.7 0.9 bitcast_add_fusion.2
  310.6 0.9 bitcast_add_fusion.2
  311.5 0.9 bitcast_add_fusion.2
  312.5 0.9 bitcast_add_fusion.2
  313.4 0.9 bitcast_add_fusion.2
  314.3 0.9 bitcast_add_fusion.2
  315.3 0.9 bitcast_add_fusion.2
  316.2 0.9 bitcast_add_fusion.2
  317.1 0.9 bitcast_add_fusion.2
  318.2 1.9 add_multiply_fusion
  320.1 1.0 fusion.10
  321.1 6.3 %copy.84 = f32[16,16,1024]{0,1,2:T(8,128)} copy(f32[16,16,1024]{2,1,0:T(8,128)S(1)} %fusion.10) | data formatting | bytes 2097152 | tf_op jit(solution)/shard_map/sto,oc->stc/dot_general | solution.py:82
  327.4 6.1 %copy.89 = f32[16,16,1024]{1,0,2:T(8,128)} copy(f32[16,16,1024]{2,1,0:T(8,128)S(1)} %get-tuple-element.76) | data formatting | bytes 2097152 | tf_op jit(solution)/shard_map/exp | solution.py:104
  333.6 6.2 %copy.90 = f32[16,16,1024]{1,0,2:T(8,128)} copy(f32[16,16,1024]{2,1,0:T(8,128)S(1)} %get-tuple-element.72) | data formatting | bytes 2097152 | tf_op jit(solution)/shard_map/mul | solution.py:106
  339.7 14.6 %fusion.14 = f32[1024,16,16]{2,1,0:T(8,128)} fusion(f32[16,16,1024]{0,1,2:T(8,128)} %copy.84, bf16[16,16,1024]{1,0,2:T(8,128)(2,1)} %copy.85), kind=kOutput, calls=%fused_computation.71 | convolution fusion | flops 50331648 | bytes 2621440 | tf_op jit(solution)/shard_map/qsc,stc->qtc/dot_general | solution.py:86
  354.3 18.0 %add_bitcast_fusion = f32[16,16,1024]{0,1,2:T(8,128)} fusion(f32[1024,16,16]{2,1,0:T(8,128)} %fusion.14, f32[16,16,1024]{1,0,2:T(8,128)S(1)} %copy-done, f32[16,16,1024]{1,0,2:T(8,128)} %copy.90), kind=kOutput, calls=%fused_computation.2 | convolution fusion | flops 50593792 | bytes 4194304 | tf_op jit(solution)/shard_map/qmc,smc->qsc/dot_general | solution.py:105
  372.3 5.5 %copy.91 = f32[16,16,1024]{2,1,0:T(8,128)S(1)} copy(f32[16,16,1024]{0,1,2:T(8,128)} %add_bitcast_fusion) | data formatting | bytes 2097152 | tf_op jit(solution)/shard_map/add | solution.py:108
  378.2 79.1 %all-gather.7.cloned.1.call-done = bf16[4096,1024]{1,0:T(8,128)(2,1)} async-done(((bf16[64,1024]{1,0:T(8,128)(2,1)}), bf16[4096,1024]{1,0:T(8,128)(2,1)}) %all-gather.7.cloned.1.call-update) | async-done | bytes 8388624 | tf_op jit(solution)/shard_map/all_gather | solution.py:111
  457.3 7.1 %fusion = bf16[4096,256]{0,1:T(8,128)(2,1)} fusion(bf16[256,1024]{1,0:T(8,128)(2,1)S(1)} %fusion.1, bf16[4096,1024]{1,0:T(8,128)(2,1)} %all-gather.7.cloned.1.call-done), kind=kOutput, calls=%fused_computation.4 | convolution fusion | flops 2148532224 | bytes 11010048 | tf_op jit(solution)/shard_map/dot_general | solution.py:110
  464.5 37.9 %reduce-scatter.2.cloned.1.call-done = bf16[512,256]{0,1:T(8,128)(2,1)} async-done(((bf16[4096,256]{0,1:T(8,128)(2,1)}), bf16[512,256]{0,1:T(8,128)(2,1)}) %reduce-scatter.2.cloned.1.call-update) | async-done | bytes 262160 | tf_op jit(solution)/shard_map/reduce_scatter | solution.py:116
  502.4 1.8 copy.92
  (69 shorter events, 3.7 us)
Async XLA Ops:
  6.5 18.9 %copy-start.2 = (bf16[256,1024]{1,0:T(8,128)(2,1)S(1)}, bf16[256,1024]{1,0:T(8,128)(2,1)}, u32[]{:S(2)}) copy-start(bf16[256,1024]{1,0:T(8,128)(2,1)} %param.11) | copy-start | bytes 1572868
  6.5 18.9 %copy-start.3 = (bf16[256,1024]{1,0:T(8,128)(2,1)S(1)}, bf16[256,1024]{1,0:T(8,128)(2,1)}, u32[]{:S(2)}) copy-start(bf16[256,1024]{1,0:T(8,128)(2,1)} %param.12) | copy-start | bytes 1572868
  6.5 152.7 %all-gather.9.cloned.1.call-start = ((), (), s32[]{:S(2)}) async-start(), calls=%async_computation.4 | async-start | bytes 4259840 | tf_op jit(solution)/shard_map/all_gather | solution.py:16
  8.2 295.0 %all-gather.5.cloned.1.call-start = ((), (), s32[]{:S(2)}) async-start(), calls=%async_computation.1 | async-start | bytes 4259840 | tf_op jit(solution)/shard_map/all_gather | solution.py:16
  9.0 16.4 %collective-permute-start.1 = (bf16[2,1024]{1,0:T(2,128)(2,1)S(1)}, bf16[2,1024]{1,0:T(2,128)(2,1)S(1)}, u32[]{:S(2)}, u32[]{:S(2)}) collective-permute-start(bf16[2,1024]{1,0:T(2,128)(2,1)S(1)} %slice.217), channel_id=1, source_target_pairs={{0,1},{1,2},{2,3},{3,4},{4,5},{5,6},{6,7},{7,8},{8,9},{9,10},{10,1... | collective-permute-start | bytes 12296 | tf_op jit(solution)/shard_map/ppermute | solution.py:11
  13.5 11.9 %collective-permute-start.2 = (bf16[2,1024]{1,0:T(2,128)(2,1)S(1)}, bf16[2,1024]{1,0:T(2,128)(2,1)S(1)}, u32[]{:S(2)}, u32[]{:S(2)}) collective-permute-start(bf16[2,1024]{1,0:T(2,128)(2,1)S(1)} %slice.227), channel_id=1, source_target_pairs={{0,1},{1,2},{2,3},{3,4},{4,5},{5,6},{6,7},{7,8},{8,9},{9,10},{10,1... | collective-permute-start | bytes 12296 | tf_op jit(solution)/shard_map/ppermute | solution.py:11
  43.3 5.3 %copy-start.1 = (f32[16,1024]{1,0:T(8,128)S(1)}, f32[16,1024]{1,0:T(8,128)}, u32[]{:S(2)}) copy-start(f32[16,1024]{1,0:T(8,128)} %param.15) | copy-start | bytes 196612
  49.2 270.9 %copy-start.5 = (f32[16,16,16]{2,1,0:T(8,128)S(1)}, f32[16,16,16]{2,1,0:T(8,128)}, u32[]{:S(2)}) copy-start(f32[16,16,16]{2,1,0:T(8,128)} %constant.42.clone) | copy-start | bytes 49156
  54.3 403.1 %all-gather.7.cloned.1.call-start = ((), (), s32[]{:S(2)}) async-start(), calls=%async_computation.2 | async-start | bytes 8519680 | tf_op jit(solution)/shard_map/all_gather | solution.py:111
  55.0 447.4 %reduce-scatter.2.cloned.1.call-start = ((), (), s32[]{:S(2)}) async-start(), calls=%async_computation.3 | async-start | bytes 2359296 | tf_op jit(solution)/shard_map/reduce_scatter | solution.py:116
  55.8 322.0 %collective-permute-start = (bf16[2,1024]{1,0:T(2,128)(2,1)S(1)}, bf16[2,1024]{1,0:T(2,128)(2,1)S(1)}, u32[]{:S(2)}, u32[]{:S(2)}) collective-permute-start(bf16[2,1024]{1,0:T(2,128)(2,1)S(1)} %slice.207), channel_id=1, source_target_pairs={{0,1},{1,2},{2,3},{3,4},{4,5},{5,6},{6,7},{7,8},{8,9},{9,10},{10,1... | collective-permute-start | bytes 12296 | tf_op jit(solution)/shard_map/ppermute | solution.py:11
  339.7 14.6 %copy-start = (f32[16,16,1024]{1,0,2:T(8,128)S(1)}, f32[16,16,1024]{1,0,2:T(8,128)}, u32[]{:S(2)}) copy-start(f32[16,16,1024]{1,0,2:T(8,128)} %copy.89) | copy-start | bytes 3145732
  372.3 5.5 %copy-start.4 = (bf16[256,1024]{1,0:T(8,128)(2,1)S(1)}, bf16[256,1024]{1,0:T(8,128)(2,1)}, u32[]{:S(2)}) copy-start(bf16[256,1024]{1,0:T(8,128)(2,1)} %param.10) | copy-start | bytes 1572868
Sparse Core Ops, SparseCore 0:
  10.3 148.9 all-gather.8
  162.2 140.8 all-gather.4
  306.1 151.1 all-gather.6
  464.6 37.6 reduce-scatter.1
where the time goes:
time: 514 us; the launch traced here: 511 us
  waiting for transfers between devices  355 us (69%)
  local copies, waits for them, and re-layouts  54.5 us (11%)
  matrix products  53.2 us (10%)
  other arithmetic  22.9 us (4%)
  between operations  13.4 us (3%)
  starting transfers between devices  11.6 us (2%)
    all_gather x2, waiting for transfers between devices, prefix(): gathered = jax.tree.map(lambda a: lax.all_gather(a, axis), part)  237 us
    all_gather x1, waiting for transfers between devices, per_device(): lax.all_gather(out_weight, 'context', axis=0, tiled=True)  79.1 us
    reduce_scatter x1, waiting for transfers between devices, per_device(): lax.psum_scatter(partial_terms.astype(jnp.bfloat16), 'tensor', scatter_di...  37.9 us
    dot_general x1, matrix products, per_device(): jnp.einsum('qmc,smc->qsc', prior * mode_scale[None], lead_powers, precisi...  18 us
    add x22, other arithmetic, compose(): return (earlier[0] * later[0], earlier[1] * later[0] + later[1])  14.8 us
    dot_general x1, matrix products, per_device(): jnp.einsum('qsc,stc->qtc', local_rows, toeplitz, precision=lax.Precision....  14.6 us
    dot_general x1, matrix products, per_device(): jnp.einsum('qsc,smc->qmc', local_rows, tail_powers, precision=lax.Precisi...  12.5 us
    ppermute x3, starting transfers between devices, passed_along(): return lax.ppermute(block, axis, route)  11.4 us
  transfers between devices with their start and end apart: 7, of which 4 were waited for; matrix products, arithmetic and copies ran while one was open for 23% of the time, Pallas kernels for 0%

commit v1 on v0

--- a/solution.py
+++ b/solution.py
@@ -108,7 +108,10 @@
     modal_out = (local_part + carried_part).reshape(row_count, chan_count)
     gated = (q_feat.astype(jnp.float32) * modal_out).astype(jnp.bfloat16)
     partial_terms = lax.dot_general(
-        lax.all_gather(out_weight, "context", axis=0, tiled=True),
+        jnp.concatenate(
+            lax.all_to_all(jnp.stack([out_weight] * lax.axis_size("context")), "context", 0, 0),
+            axis=0,
+        ),
         gated,
         (((1,), (1,)), ((), ())),
         preferred_element_type=jnp.float32,

time: 514 us -> 763 us (1.48)
  waiting for transfers between devices: 355 us -> 582 us
  starting transfers between devices: 11.6 us -> 31 us
    ppermute x3, waiting for transfers between devices: 0.01 us -> 369 us  [passed_along(): return lax.ppermute(block, axis, route)]
    all_gather x2, waiting for transfers between devices: 237 us -> 136 us  [prefix(): gathered = jax.tree.map(lambda a: lax.all_gather(a, axis), part)]
    all_gather x1 -> x0, waiting for transfers between devices: 79.1 us -> none  [per_device(): lax.all_gather(out_weight, 'context', axis=0, tiled=True)]
    reduce_scatter x1, waiting for transfers between devices: 37.9 us -> 77.5 us  [per_device(): lax.psum_scatter(partial_terms.astype(jnp.bfloat16), 'tensor', scatter_di...]
    all_to_all x0 -> x1, starting transfers between devices: none -> 19.1 us  [per_device(): lax.all_to_all(jnp.stack([out_weight] * lax.axis_size('context')), 'conte...]
  transfers between devices with their start and end apart: 7 -> 7, of which waited for: 4 -> 4; matrix products, arithmetic and copies ran while one was open for 23% -> 16% of each run, Pallas kernels for 0% -> 0%
where the time goes in v1:
time: 763 us; the launch traced here: 760 us
  waiting for transfers between devices  582 us (76%)
  local copies, waits for them, and re-layouts  58.2 us (8%)
  matrix products  53.1 us (7%)
  starting transfers between devices  31 us (4%)
  other arithmetic  21.2 us (3%)
  between operations  13.5 us (2%)
    ppermute x3, waiting for transfers between devices, passed_along(): return lax.ppermute(block, axis, route)  369 us
    all_gather x2, waiting for transfers between devices, prefix(): gathered = jax.tree.map(lambda a: lax.all_gather(a, axis), part)  136 us
    reduce_scatter x1, waiting for transfers between devices, per_device(): lax.psum_scatter(partial_terms.astype(jnp.bfloat16), 'tensor', scatter_di...  77.5 us
    all_to_all x1, starting transfers between devices, per_device(): lax.all_to_all(jnp.stack([out_weight] * lax.axis_size('context')), 'conte...  19.1 us
    dot_general x1, matrix products, per_device(): jnp.einsum('qmc,smc->qsc', prior * mode_scale[None], lead_powers, precisi...  18 us
  transfers between devices with their start and end apart: 7, of which 4 were waited for; matrix products, arithmetic and copies ran while one was open for 16% of the time, Pallas kernels for 0%

profile of v1, /device:TPU:8, one launch (start us, length us, event | category | flops | bytes accessed | tf_op | source)
XLA Modules:
  0.0 759.7 jit_solution(6595331142446124737)
XLA Ops:
  6.5 5.2 stack.2
  11.8 19.1 %all-to-all-start = ((bf16[64,64,1024]{2,1,0:T(8,128)(2,1)}), bf16[64,64,1024]{2,1,0:T(8,128)(2,1)}, u32[]{:S(2)}, u32[]{:S(2)}) async-start(bf16[64,64,1024]{2,1,0:T(8,128)(2,1)} %stack.2), calls=%async_computation | async-start | bytes 16777216 | tf_op jit(solution)/shard_map/all_to_all | solution.py:112
  30.9 0.7 multiply_exponential_fusion.2
  31.7 3.4 collective-permute-start.1
  35.1 3.4 collective-permute-start.2
  38.5 0.2 multiply_exponential_fusion
  39.7 6.2 copy.86
  45.8 368.7 %collective-permute-done.1 = bf16[2,1024]{1,0:T(2,128)(2,1)S(1)} collective-permute-done((bf16[2,1024]{1,0:T(2,128)(2,1)S(1)}, bf16[2,1024]{1,0:T(2,128)(2,1)S(1)}, u32[]{:S(2)}, u32[]{:S(2)}) %collective-permute-start.1) | collective-permute-done | bytes 4128 | tf_op jit(solution)/shard_map/ppermute | solution.py:11
  414.6 0.7 multiply_convert_fusion
  415.4 4.7 copy.85
  420.1 12.5 %fusion.15 = f32[1024,16,16]{1,2,0:T(8,128)} fusion(f32[16,16,1024]{1,0,2:T(8,128)} %copy.86, bf16[16,16,1024]{1,0,2:T(8,128)(2,1)} %copy.85), kind=kOutput, calls=%fused_computation.72 | convolution fusion | flops 50331648 | bytes 2621440 | tf_op jit(solution)/shard_map/qsc,smc->qmc/dot_general | solution.py:88
  432.6 5.1 copy.88
  438.4 3.5 pad.122
  441.9 1.5 slice.359
  443.4 0.7 slice.207
  444.2 5.1 collective-permute-start
  449.8 3.5 pad.33
  453.6 2.3 slice_add_fusion
  455.9 135.7 %all-gather.4.cloned.1.call-done = f32[64,16,1024]{2,1,0:T(8,128)} async-done(((f32[1,16,1024]{2,1,0:T(8,128)}), f32[64,16,1024]{2,1,0:T(8,128)}) %all-gather.4.cloned.1.call-update) | async-done | bytes 4194320 | tf_op jit(solution)/shard_map/all_gather | solution.py:16
  591.5 15.0 %while.12 = (s32[]{:T(128)}, f32[16,1024]{1,0:T(8,128)S(1)}, s32[]{:T(128)}, f32[64,16,1024]{2,1,0:T(8,128)}, f32[64,16,1024]{2,1,0:T(8,128)}, /*index=5*/s32[]{:T(128)}, s32[]{:T(128)}, s32[]{:T(128)}) while((s32[]{:T(128)}, f32[16,1024]{1,0:T(8,128)S(1)}, s32[]{:T(128)}, f32[64,16,1024]{2,1,0:T(8,128)}, f32[64,16,1024]{2,1,0:T(8,128)}, ...), condition=%wide.region_2.3_spmd, body=%wide.region_1.2_spmd.sunk | while | flops 32773 | bytes 262267 | solution.py:24
  591.5 0.9 bitcast_add_fusion.2
  592.5 0.9 bitcast_add_fusion.2
  593.4 0.9 bitcast_add_fusion.2
  594.3 0.9 bitcast_add_fusion.2
  595.3 0.9 bitcast_add_fusion.2
  596.2 0.9 bitcast_add_fusion.2
  597.1 0.9 bitcast_add_fusion.2
  598.1 0.9 bitcast_add_fusion.2
  599.0 0.9 bitcast_add_fusion.2
  599.9 0.9 bitcast_add_fusion.2
  600.8 0.9 bitcast_add_fusion.2
  601.8 0.9 bitcast_add_fusion.2
  602.7 0.9 bitcast_add_fusion.2
  603.6 0.9 bitcast_add_fusion.2
  604.6 0.9 bitcast_add_fusion.2
  605.5 0.9 bitcast_add_fusion.2
  606.6 1.9 add_multiply_fusion
  608.5 1.0 fusion.10
  609.5 6.3 copy.84
  615.8 6.2 copy.89
  622.0 6.2 copy.90
  628.2 14.6 %fusion.14 = f32[1024,16,16]{2,1,0:T(8,128)} fusion(f32[16,16,1024]{0,1,2:T(8,128)} %copy.84, bf16[16,16,1024]{1,0,2:T(8,128)(2,1)} %copy.85), kind=kOutput, calls=%fused_computation.71 | convolution fusion | flops 50331648 | bytes 2621440 | tf_op jit(solution)/shard_map/qsc,stc->qtc/dot_general | solution.py:86
  642.7 18.0 %add_bitcast_fusion = f32[16,16,1024]{0,1,2:T(8,128)} fusion(f32[1024,16,16]{2,1,0:T(8,128)} %fusion.14, f32[16,16,1024]{1,0,2:T(8,128)S(1)} %copy-done, f32[16,16,1024]{1,0,2:T(8,128)} %copy.90), kind=kOutput, calls=%fused_computation.2 | convolution fusion | flops 50593792 | bytes 4194304 | tf_op jit(solution)/shard_map/qmc,smc->qsc/dot_general | solution.py:105
  660.7 5.5 copy.91
  666.2 0.4 fusion.1
  666.6 7.2 fusion
  673.8 77.5 %reduce-scatter.2.cloned.1.call-done = bf16[512,256]{0,1:T(8,128)(2,1)} async-done(((bf16[4096,256]{0,1:T(8,128)(2,1)}), bf16[512,256]{0,1:T(8,128)(2,1)}) %reduce-scatter.2.cloned.1.call-update) | async-done | bytes 262160 | tf_op jit(solution)/shard_map/reduce_scatter | solution.py:119
  751.3 1.8 copy.92
  (73 shorter events, 2.6 us)
Async XLA Ops:
  11.7 19.1 %copy-start.1 = (f32[16,1024]{1,0:T(8,128)S(1)}, f32[16,1024]{1,0:T(8,128)}, u32[]{:S(2)}) copy-start(f32[16,1024]{1,0:T(8,128)} %param.15) | copy-start | bytes 196612
  11.7 19.2 %copy-start.6 = (f32[16,1024]{1,0:T(8,128)S(1)}, f32[16,1024]{1,0:T(8,128)}, u32[]{:S(2)}) copy-start(f32[16,1024]{1,0:T(8,128)} %param.14) | copy-start | bytes 196612
  11.7 19.9 %copy-start.2 = (bf16[256,1024]{1,0:T(8,128)(2,1)S(1)}, bf16[256,1024]{1,0:T(8,128)(2,1)}, u32[]{:S(2)}) copy-start(bf16[256,1024]{1,0:T(8,128)(2,1)} %param.11) | copy-start | bytes 1572868
  11.7 23.3 %copy-start.3 = (bf16[256,1024]{1,0:T(8,128)(2,1)S(1)}, bf16[256,1024]{1,0:T(8,128)(2,1)}, u32[]{:S(2)}) copy-start(bf16[256,1024]{1,0:T(8,128)(2,1)} %param.12) | copy-start | bytes 1572868
  11.7 26.7 %copy-start.7 = (bf16[3,3,64]{2,1,0:T(4,128)(2,1)S(1)}, bf16[3,3,64]{2,1,0:T(4,128)(2,1)}, u32[]{:S(2)}) copy-start(bf16[3,3,64]{2,1,0:T(4,128)(2,1)} %param.13) | copy-start | bytes 3460
  11.8 654.9 %all-to-all-start = ((bf16[64,64,1024]{2,1,0:T(8,128)(2,1)}), bf16[64,64,1024]{2,1,0:T(8,128)(2,1)}, u32[]{:S(2)}, u32[]{:S(2)}) async-start(bf16[64,64,1024]{2,1,0:T(8,128)(2,1)} %stack.2), calls=%async_computation | async-start | bytes 16777216 | tf_op jit(solution)/shard_map/all_to_all | solution.py:112
  30.8 425.1 %all-gather.6.cloned.1.call-start = ((), (), s32[]{:S(2)}) async-start(), calls=%async_computation.4 | async-start | bytes 4259840 | tf_op jit(solution)/shard_map/all_gather | solution.py:16
  31.6 559.9 %all-gather.4.cloned.1.call-start = ((), (), s32[]{:S(2)}) async-start(), calls=%async_computation.2 | async-start | bytes 4259840 | tf_op jit(solution)/shard_map/all_gather | solution.py:16
  31.7 382.8 %collective-permute-start.1 = (bf16[2,1024]{1,0:T(2,128)(2,1)S(1)}, bf16[2,1024]{1,0:T(2,128)(2,1)S(1)}, u32[]{:S(2)}, u32[]{:S(2)}) collective-permute-start(bf16[2,1024]{1,0:T(2,128)(2,1)S(1)} %slice.217), channel_id=1, source_target_pairs={{0,1},{1,2},{2,3},{3,4},{4,5},{5,6},{6,7},{7,8},{8,9},{9,10},{10,1... | collective-permute-start | bytes 12296 | tf_op jit(solution)/shard_map/ppermute | solution.py:11
  35.1 379.5 %collective-permute-start.2 = (bf16[2,1024]{1,0:T(2,128)(2,1)S(1)}, bf16[2,1024]{1,0:T(2,128)(2,1)S(1)}, u32[]{:S(2)}, u32[]{:S(2)}) collective-permute-start(bf16[2,1024]{1,0:T(2,128)(2,1)S(1)} %slice.227), channel_id=1, source_target_pairs={{0,1},{1,2},{2,3},{3,4},{4,5},{5,6},{6,7},{7,8},{8,9},{9,10},{10,1... | collective-permute-start | bytes 12296 | tf_op jit(solution)/shard_map/ppermute | solution.py:11
  438.4 170.1 %copy-start.5 = (f32[16,16,16]{2,1,0:T(8,128)S(1)}, f32[16,16,16]{2,1,0:T(8,128)}, u32[]{:S(2)}) copy-start(f32[16,16,16]{2,1,0:T(8,128)} %constant.42.clone) | copy-start | bytes 49156
  443.4 308.0 %reduce-scatter.2.cloned.1.call-start = ((), (), s32[]{:S(2)}) async-start(), calls=%async_computation.3 | async-start | bytes 2359296 | tf_op jit(solution)/shard_map/reduce_scatter | solution.py:119
  444.2 222.0 %collective-permute-start = (bf16[2,1024]{1,0:T(2,128)(2,1)S(1)}, bf16[2,1024]{1,0:T(2,128)(2,1)S(1)}, u32[]{:S(2)}, u32[]{:S(2)}) collective-permute-start(bf16[2,1024]{1,0:T(2,128)(2,1)S(1)} %slice.207), channel_id=1, source_target_pairs={{0,1},{1,2},{2,3},{3,4},{4,5},{5,6},{6,7},{7,8},{8,9},{9,10},{10,1... | collective-permute-start | bytes 12296 | tf_op jit(solution)/shard_map/ppermute | solution.py:11
  628.2 14.6 %copy-start = (f32[16,16,1024]{1,0,2:T(8,128)S(1)}, f32[16,16,1024]{1,0,2:T(8,128)}, u32[]{:S(2)}) copy-start(f32[16,16,1024]{1,0,2:T(8,128)} %copy.89) | copy-start | bytes 3145732
  660.7 5.5 copy-start.4
Sparse Core Ops, SparseCore 0:
  34.6 234.4 all-gather.5
  443.5 147.9 all-gather.3
  673.9 77.3 reduce-scatter.1
